TPU v7x, 256 devices: a whole 4x4x8 slice. The times are simulated.
256 devices in a mesh: dp: 2 (over core), context: 32 (over x, z), tensor: 4 (over y).
Axes of the slice: x: 4, y: 4, z: 8, core: 2. Of those that a mesh axis runs over, the one named last changes fastest.
Arguments:
- query_rows: bfloat16 [2, 8192, 4096], P('dp', 'context', 'tensor'), may hold values from -6 to 6
- key_rows: bfloat16 [2, 8192, 4096], P('dp', 'context', 'tensor'), may hold values from -6 to 6
- value_rows: bfloat16 [2, 8192, 4096], P('dp', 'context', 'tensor'), may hold values from -6 to 6
- filters: bfloat16 [256, 128], P('tensor'), may hold values from -0.5 to 0.5
- out_weight: bfloat16 [4096, 4096], P('tensor'), may hold values from -0.09375 to 0.09375
- lengths: int32 [2, 32], P('dp'), may hold values from 1 to 512, 8192 in all within a row
- panel_plan: int32 [2, 1024], P('dp'), may hold values from 0 to 1023, as said below
- out_grad: bfloat16 [2, 8192, 4096], P('dp', 'context', 'tensor'), may hold values from -6 to 6
Outputs:
- mixed: bfloat16 [2, 8192, 4096], P('dp', 'context', 'tensor')
- query_grad: bfloat16 [2, 8192, 4096], P('dp', 'context', 'tensor')
- key_grad: bfloat16 [2, 8192, 4096], P('dp', 'context', 'tensor')
- value_grad: bfloat16 [2, 8192, 4096], P('dp', 'context', 'tensor')
- filter_grad: float32 [256, 128], P('tensor')
Inputs may be any that keep to these rules, and one draw needn't show every extreme that they name: Each row of panel_plan is a permutation of 0 to 1023, and within each aligned block of 32 entries (the panels of one loader index of context) the values divided by 32, rounded down, are a permutation of 0 to 31. `lengths`: each row sums to 8192.
All inputs are finite; a program needn't handle non-finite values.
Results may differ from a plain program's by a relative error of at most 0.009.
Values may be sent and summed in bfloat16 or wider, within the bound.
A program may use at most 128 MiB of HBM per device.

v0:
```python
import math
import jax
import jax.numpy as jnp
from jax import lax
from jax.sharding import Mesh
from jax.sharding import PartitionSpec as P

CONTEXT = ("context_0", "context_1")
DP_CONTEXT = ("dp", "context_0", "context_1")


def sent_together(arrays, axis, split_dim, concat_dim, along):
    widths = [a.shape[along] for a in arrays]
    both = jnp.concatenate(arrays, axis=along)
    out = lax.all_to_all(both, axis, split_axis=split_dim, concat_axis=concat_dim, tiled=True)
    return tuple(jnp.split(out, [sum(widths[:k]) for k in range(1, len(widths))], axis=along))


def from_behind(value, axis, steps):
    count = lax.axis_size(axis)
    first, last = (max(0, -steps), min(count, count - steps))
    return lax.ppermute(value, axis, [(source, source + steps) for source in range(first, last)])


def in_blocks(shard, dim, length):
    before, after = (shard.shape[:dim], shard.shape[dim + 1 :])
    return jnp.moveaxis(shard.reshape(*before, length, -1, *after), dim, 0)


def summed_on_arrival(shard, axis, dim):
    blocks = in_blocks(shard, dim, lax.axis_size(axis))
    arrived = lax.all_to_all(blocks, axis, split_axis=0, concat_axis=0, tiled=True)
    return arrived.astype(jnp.float32).sum(axis=0)


def from_everyone(shard, axis):
    copies = jnp.broadcast_to(shard, (lax.axis_size(axis), *shard.shape))
    return lax.all_to_all(copies, axis, split_axis=0, concat_axis=0, tiled=True)


def laid_out(blocks, dim):
    shape = list(blocks.shape[1:])
    shape[dim] *= blocks.shape[0]
    return jnp.moveaxis(blocks, 0, dim).reshape(shape)


def collect(shard, axis, dim):
    blocks = from_everyone(shard, axis)
    return laid_out(blocks, dim)


def over_axes(shard, axes):
    for axis in axes:
        shard = lax.psum(shard, axis)
    return shard


def regroup(matrix, rows_in):
    count = matrix.shape[1]
    flat = rows_in.reshape(count, -1)
    moved = jnp.dot(matrix, flat, preferred_element_type=jnp.float32)
    return moved.astype(jnp.bfloat16).reshape(rows_in.shape)


def doc_ages(positions, lengths_row):
    starts = jnp.cumsum(lengths_row) - lengths_row
    begin = jnp.max(jnp.where(starts[None, :] <= positions[:, None], starts[None, :], 0), axis=1)
    return positions - begin


def band_matrix(filters, tap_table):
    groups, taps = filters.shape
    flat = jnp.dot(filters, tap_table.reshape(taps, -1), preferred_element_type=jnp.float32)
    return flat.astype(jnp.bfloat16).reshape(groups, 2 * taps, taps)


def time_major(rows, groups, taps):
    total, width = rows.shape
    columns = rows.T.reshape(groups, width // groups, total)
    head = columns[:, :, : total - taps].reshape(groups, width // groups, -1, taps)
    tail = columns[:, :, taps:].reshape(groups, width // groups, -1, taps)
    return (head, tail)


def per_device(
    query_rows, key_rows, value_rows, filters, out_weight, lengths, panel_plan, out_grad
):
    groups, taps = filters.shape
    length, width = (query_rows.shape[1], query_rows.shape[2])
    block_count = length // taps
    panel_count = lax.axis_size(CONTEXT)
    device_rank = lax.axis_index(CONTEXT)
    plan_rows = panel_plan[0].reshape(panel_count, panel_count)
    own_plan = lax.dynamic_slice_in_dim(plan_rows, device_rank, 1, 0)[0]
    slot_ids = jnp.arange(panel_count, dtype=jnp.int32)
    select = (own_plan[None, :] // panel_count == slot_ids[:, None]).astype(jnp.bfloat16)
    sender_slot = jnp.sum(
        jnp.where(plan_rows // panel_count == device_rank, plan_rows % panel_count, 0), axis=1
    )
    placing = (sender_slot[None, :] == slot_ids[:, None]).astype(jnp.bfloat16)
    local_product = (key_rows[0].astype(jnp.float32) * value_rows[0].astype(jnp.float32)).astype(
        jnp.bfloat16
    )
    arrived = sent_together(
        (regroup(select, query_rows[0]), regroup(select, local_product)), CONTEXT, 0, 0, 1
    )
    query_own = regroup(placing, arrived[0])
    product = regroup(placing, arrived[1])
    tap_ids = jnp.arange(taps, dtype=jnp.int32)
    out_ids = jnp.arange(taps, dtype=jnp.int32)
    win_ids = jnp.arange(2 * taps, dtype=jnp.int32)
    fwd_lag = out_ids[None, :] + taps - win_ids[:, None]
    bwd_lag = win_ids[:, None] - out_ids[None, :]
    fwd_table = (fwd_lag[None] == tap_ids[:, None, None]).astype(jnp.bfloat16)
    bwd_table = (bwd_lag[None] == tap_ids[:, None, None]).astype(jnp.bfloat16)
    fwd_band = band_matrix(filters, fwd_table)
    bwd_band = band_matrix(filters, bwd_table)
    positions = device_rank * length + jnp.arange(length + taps, dtype=jnp.int32)
    age_all = doc_ages(positions, lengths[0])
    age_here = age_all[:length].reshape(block_count, taps)
    age_windows = jnp.concatenate(
        [age_all[:length].reshape(block_count, taps), age_all[taps:].reshape(block_count, taps)],
        axis=1,
    )
    fwd_mask = fwd_lag[None] <= age_here[:, None, :]
    bwd_mask = bwd_lag[None] <= age_windows[:, :, None]
    rim_rows = from_behind(product[length - taps + 1 :], CONTEXT, 1)
    padded = jnp.concatenate([jnp.zeros((1, width), jnp.bfloat16), rim_rows, product], axis=0)
    prod_head, prod_tail = time_major(padded, groups, taps)
    masked = fwd_band[None] * fwd_mask[:, None].astype(jnp.bfloat16)
    conv_cols = jnp.einsum(
        "gcks,kgst->gckt", prod_head, masked[:, :, :taps], preferred_element_type=jnp.float32
    )
    conv_cols = conv_cols + jnp.einsum(
        "gcks,kgst->gckt", prod_tail, masked[:, :, taps:], preferred_element_type=jnp.float32
    )
    conv = conv_cols.reshape(width, length).T
    gated = (query_own.astype(jnp.float32) * conv).astype(jnp.bfloat16)
    partial_value = jnp.dot(gated, out_weight, preferred_element_type=jnp.float32)
    mixed = summed_on_arrival(partial_value.astype(jnp.bfloat16), "tensor", 1).astype(jnp.bfloat16)[
        None
    ]
    grad_gated = lax.dot_general(
        collect(out_grad[0], "tensor", 1),
        out_weight,
        (((1,), (1,)), ((), ())),
        preferred_element_type=jnp.float32,
    )
    query_back = (grad_gated * conv).astype(jnp.bfloat16)
    conv_back = (grad_gated * query_own.astype(jnp.float32)).astype(jnp.bfloat16)
    rim_back = from_behind(conv_back[: taps - 1], CONTEXT, -1)
    padded_back = jnp.concatenate(
        [conv_back, rim_back, jnp.zeros((1, width), jnp.bfloat16)], axis=0
    )
    back_head, back_tail = time_major(padded_back, groups, taps)
    back_masked = bwd_band[None] * bwd_mask[:, None].astype(jnp.bfloat16)
    back_cols = jnp.einsum(
        "gckt,kgts->gcks", back_head, back_masked[:, :, :taps], preferred_element_type=jnp.float32
    )
    back_cols = back_cols + jnp.einsum(
        "gckt,kgts->gcks", back_tail, back_masked[:, :, taps:], preferred_element_type=jnp.float32
    )
    product_back = back_cols.reshape(width, length).T.astype(jnp.bfloat16)
    mask_float = fwd_mask.astype(jnp.float32)
    outer_head = jnp.einsum(
        "gcks,gckt->kgst", prod_head, back_head, preferred_element_type=jnp.float32
    )
    outer_tail = jnp.einsum(
        "gcks,gckt->kgst", prod_tail, back_head, preferred_element_type=jnp.float32
    )
    summed_head = jnp.sum(outer_head * mask_float[:, None, :taps], axis=0).reshape(
        groups, taps * taps
    )
    summed_tail = jnp.sum(outer_tail * mask_float[:, None, taps:], axis=0).reshape(
        groups, taps * taps
    )
    table_float = fwd_table.astype(jnp.float32)
    table_head = table_float[:, :taps].reshape(taps, taps * taps)
    table_tail = table_float[:, taps:].reshape(taps, taps * taps)
    dims = (((1,), (1,)), ((), ()))
    tap_sums = lax.dot_general(
        summed_head,
        table_head,
        dims,
        precision=lax.Precision.HIGHEST,
        preferred_element_type=jnp.float32,
    )
    tap_sums = tap_sums + lax.dot_general(
        summed_tail,
        table_tail,
        dims,
        precision=lax.Precision.HIGHEST,
        preferred_element_type=jnp.float32,
    )
    total_tokens = lax.axis_size("dp") * panel_count * length
    scale = 1.0 / math.sqrt(float(total_tokens))
    filter_grad = over_axes(tap_sums * scale, DP_CONTEXT)
    back_placing = placing.T
    back_select = select.T
    returned = sent_together(
        (regroup(back_placing, query_back), regroup(back_placing, product_back)), CONTEXT, 0, 0, 1
    )
    query_grad = regroup(back_select, returned[0])
    product_home = regroup(back_select, returned[1]).astype(jnp.float32)
    key_grad = (product_home * value_rows[0].astype(jnp.float32)).astype(jnp.bfloat16)
    value_grad = (product_home * key_rows[0].astype(jnp.float32)).astype(jnp.bfloat16)
    return (mixed, query_grad[None], key_grad[None], value_grad[None], filter_grad)


def solution(mesh):
    finer = Mesh(
        mesh.devices.reshape(mesh.shape["dp"], 4, 8, mesh.shape["tensor"]),
        ("dp", "context_0", "context_1", "tensor"),
    )
    in_specs = (
        P("dp", CONTEXT, "tensor"),
        P("dp", CONTEXT, "tensor"),
        P("dp", CONTEXT, "tensor"),
        P("tensor", None),
        P("tensor", None),
        P("dp", None),
        P("dp", None),
        P("dp", CONTEXT, "tensor"),
    )
    out_specs = (
        P("dp", CONTEXT, "tensor"),
        P("dp", CONTEXT, "tensor"),
        P("dp", CONTEXT, "tensor"),
        P("dp", CONTEXT, "tensor"),
        P("tensor", None),
    )
    return jax.shard_map(
        per_device, mesh=finer, in_specs=in_specs, out_specs=out_specs, check_vma=False
    )
```

profile of v0, /device:TPU:8, one launch (start us, length us, event | category | flops | bytes accessed | tf_op | source)
XLA Modules:
  0.0 220.8 jit_solution(11974155271854987153)
XLA Ops:
  6.8 12.0 %all-to-all-start = ((bf16[32,8,2048]{2,1,0:T(8,128)(2,1)}), bf16[32,8,2048]{2,1,0:T(8,128)(2,1)}, u32[]{:S(2)}, u32[]{:S(2)}) async-start(bf16[32,8,2048]{2,1,0:T(8,128)(2,1)} %pad_maximum_fusion), calls=%async_computation | async-start | bytes 2097152 | tf_op jit(solution)/shard_map/all_to_all | solution.py:15
  20.0 3.9 %fusion.18 = bf16[8,8,256,128]{3,1,2,0:T(8,128)(2,1)S(1)} fusion(bf16[64,128]{1,0:T(8,128)(2,1)S(1)} %copy-done, s32[32768]{0:T(1024)S(1)} %get-tuple-element.23), kind=kOutput, calls=%fused_computation.36 | convolution fusion | flops 543162368 | bytes 4341760 | tf_op jit(solution)/shard_map/dot_general | solution.py:73
  24.7 5.9 %fusion.19 = bf16[8,8,256,128]{3,1,2,0:T(8,128)(2,1)} fusion(bf16[64,128]{1,0:T(8,128)(2,1)S(1)} %copy-done, s32[32768]{0:T(1024)S(1)} %fusion.77), kind=kOutput, calls=%fused_computation.37 | convolution fusion | flops 543162368 | bytes 4341760 | tf_op jit(solution)/shard_map/dot_general | solution.py:73
  31.7 3.1 %copy.95 = bf16[8,8,256,128]{3,2,1,0:T(8,128)(2,1)} copy(bf16[8,8,256,128]{3,1,2,0:T(8,128)(2,1)S(1)} %fusion.18) | data formatting | bytes 8388608
  35.1 5.4 %copy.98 = bf16[8,8,256,128]{3,2,1,0:T(8,128)(2,1)} copy(bf16[8,8,256,128]{3,1,2,0:T(8,128)(2,1)} %fusion.19) | data formatting | bytes 8388608
  40.6 4.7 %broadcast_multiply_fusion.1 = bf16[2,64,256,128]{3,2,0,1:T(8,128)(2,1)} fusion(bf16[2,256,128]{2,1,0:T(8,128)(2,1)} %get-tuple-element.20, bf16[64,256,128]{2,1,0:T(8,128)(2,1)S(1)} %bitcast.132), kind=kLoop, calls=%fused_computation.35 | loop fusion | flops 4194304 | bytes 12713984 | tf_op jit(solution)/shard_map/mul | solution.py:130
  45.3 6.0 %broadcast_multiply_fusion = bf16[2,64,256,128]{3,2,0,1:T(8,128)(2,1)} fusion(bf16[2,256,128]{2,1,0:T(8,128)(2,1)} %compare_convert_fusion.2, bf16[64,256,128]{2,1,0:T(8,128)(2,1)} %bitcast.133), kind=kLoop, calls=%fused_computation.34 | loop fusion | flops 4194304 | bytes 12713984 | tf_op jit(solution)/shard_map/mul | solution.py:156
  52.8 4.9 %all-to-all-start.2 = ((bf16[4,256,1024]{1,2,0:T(8,128)(2,1)}), bf16[4,256,1024]{1,2,0:T(8,128)(2,1)}, u32[]{:S(2)}, u32[]{:S(2)}) async-start(bf16[4,256,1024]{1,2,0:T(8,128)(2,1)} %broadcast_in_dim.14), calls=%async_computation.2 | async-start | bytes 4194304 | tf_op jit(solution)/shard_map/all_to_all | solution.py:38
  60.2 4.0 %collective-permute-start = (bf16[127,1024]{0,1:T(8,128)(2,1)S(1)}, bf16[127,1024]{0,1:T(8,128)(2,1)S(1)}, u32[]{:S(2)}, u32[]{:S(2)}) collective-permute-start(bf16[127,1024]{0,1:T(8,128)(2,1)S(1)} %slice.71), channel_id=1, source_target_pairs={{0,4},{4,8},{8,12},{12,16},{16,20},{20,24},{24,28},{28,32},{32,36}... | collective-permute-start | bytes 780296 | tf_op jit(solution)/shard_map/ppermute | solution.py:22
  65.6 3.1 %collective-permute-done = bf16[127,1024]{0,1:T(8,128)(2,1)S(1)} collective-permute-done((bf16[127,1024]{0,1:T(8,128)(2,1)S(1)}, bf16[127,1024]{0,1:T(8,128)(2,1)S(1)}, u32[]{:S(2)}, u32[]{:S(2)}) %collective-permute-start) | collective-permute-done | bytes 260128 | tf_op jit(solution)/shard_map/ppermute | solution.py:22
  69.9 3.4 %fusion.12 = f32[64,2,128,16]{2,3,1,0:T(8,128)S(1)} fusion(bf16[2,64,256,128]{3,2,0,1:T(8,128)(2,1)} %broadcast_multiply_fusion.1, bf16[64,2,2,8,128]{4,3,2,1,0:T(8,128)(2,1)S(1)} %get-tuple-element.16), kind=kOutput, calls=%fused_computation.28 | convolution fusion | flops 67108864 | bytes 5767168 | tf_op jit(solution)/shard_map/gcks,kgst->gckt/dot_general | solution.py:134
  73.3 3.4 %fusion.23 = f32[64,16,2,128]{3,1,2,0:T(8,128)S(1)} fusion(f32[64,2,128,16]{2,3,1,0:T(8,128)S(1)} %fusion.12, bf16[2,64,256,128]{3,2,0,1:T(8,128)(2,1)} %broadcast_multiply_fusion.1, bf16[64,2,2,8,128]{4,3,2,1,0:T(8,128)(2,1)S(1)} %get-tuple-element.15), kind=kOutput, calls=%fused_computation.40 | convolution fusion | flops 67371008 | bytes 6815744 | tf_op jit(solution)/shard_map/gcks,kgst->gckt/dot_general | solution.py:131
  78.8 3.9 %all-to-all-done.2 = bf16[4,256,1024]{1,2,0:T(8,128)(2,1)} async-done(((bf16[4,256,1024]{1,2,0:T(8,128)(2,1)}), bf16[4,256,1024]{1,2,0:T(8,128)(2,1)}, u32[]{:S(2)}, u32[]{:S(2)}) %all-to-all-start.2) | async-done | bytes 2097184 | tf_op jit(solution)/shard_map/all_to_all | solution.py:38
  82.7 7.5 %fusion.59 = (bf16[256,1024]{1,0:T(8,128)(2,1)}, bf16[256,1024]{1,0:T(8,128)(2,1)S(1)}) fusion(f32[1024,256]{0,1:T(8,128)} %copy.70, f32[256,1024]{1,0:T(8,128)S(1)} %reshape.225, bf16[256,4096]{0,1:T(8,128)(2,1)} %bitcast.16, bf16[1024,4096]{1,0:T(8,128)(2,1)} %param.12), kind=kOutput, calls=%fused_computation.60 | convolution fusion | flops 2148532224 | bytes 13631488 | tf_op jit(solution)/shard_map/dot_general | solution.py:143
  92.5 6.1 %convolution_convert_fusion.10 = bf16[256,4096]{1,0:T(8,128)(2,1)S(1)} fusion(bf16[1024,4096]{1,0:T(8,128)(2,1)} %param.12, f32[256,1024]{1,0:T(8,128)} %copy-done.9, f32[1024,256]{0,1:T(8,128)S(1)} %copy-done.10), kind=kOutput, calls=%fused_computation.23 | convolution fusion | flops 2149056512 | bytes 12582912 | tf_op jit(solution)/shard_map/dot_general | solution.py:139
  102.9 5.0 %all-to-all-start.1 = ((bf16[4,256,1024]{2,1,0:T(8,128)(2,1)}), bf16[4,256,1024]{2,1,0:T(8,128)(2,1)S(1)}, u32[]{:S(2)}, u32[]{:S(2)}) async-start(bf16[4,256,1024]{2,1,0:T(8,128)(2,1)} %bitcast.134), calls=%async_computation.1 | async-start | bytes 4194304 | tf_op jit(solution)/shard_map/all_to_all | solution.py:32
  113.5 3.4 %fusion.8 = f32[64,2,128,16]{2,3,1,0:T(8,128)S(1)} fusion(bf16[2,64,256,128]{3,2,0,1:T(8,128)(2,1)} %broadcast_multiply_fusion, bf16[64,2,2,8,128]{4,3,2,1,0:T(8,128)(2,1)S(1)} %get-tuple-element.14), kind=kOutput, calls=%fused_computation.24 | convolution fusion | flops 67108864 | bytes 5767168 | tf_op jit(solution)/shard_map/gckt,kgts->gcks/dot_general | solution.py:160
  117.0 3.4 %fusion.32 = bf16[64,16,2,128]{3,1,2,0:T(8,128)(2,1)S(1)} fusion(f32[64,2,128,16]{2,3,1,0:T(8,128)S(1)} %fusion.8, bf16[2,64,256,128]{3,2,0,1:T(8,128)(2,1)} %broadcast_multiply_fusion, bf16[64,2,2,8,128]{4,3,2,1,0:T(8,128)(2,1)S(1)} %get-tuple-element.13), kind=kOutput, calls=%fused_computation.46 | convolution fusion | flops 67633152 | bytes 6291456 | tf_op jit(solution)/shard_map/gckt,kgts->gcks/dot_general | solution.py:157
  131.8 10.6 %all-to-all-start.3 = ((bf16[32,8,2048]{2,1,0:T(8,128)(2,1)}), bf16[32,8,2048]{2,1,0:T(8,128)(2,1)}, u32[]{:S(2)}, u32[]{:S(2)}) async-start(bf16[32,8,2048]{2,1,0:T(8,128)(2,1)} %pad_maximum_fusion.1), calls=%async_computation.3 | async-start | bytes 2097152 | tf_op jit(solution)/shard_map/all_to_all | solution.py:15
  148.2 6.4 %fusion.35 = f32[64,128]{1,0:T(8,128)S(1)} fusion(pred[128,256,128]{2,0,1:T(32,128)(4,1)S(1)} %iota_compare_fusion, f32[64,128,128]{2,1,0:T(8,128)S(1)} %multiply_reduce_fusion.1), kind=kOutput, calls=%fused_computation.47 | convolution fusion | flops 1610612736 | bytes 6324224 | tf_op jit(solution)/shard_map/dot_general | solution.py:181
  154.6 6.8 %fusion.50 = f32[64,128]{1,0:T(8,128)S(1)} fusion(f32[64,128]{1,0:T(8,128)S(1)} %fusion.35, pred[128,256,128]{2,0,1:T(32,128)(4,1)S(1)} %iota_compare_fusion, f32[64,128,128]{2,1,0:T(8,128)S(1)} %multiply_reduce_fusion), kind=kOutput, calls=%fused_computation.50 | convolution fusion | flops 1610629120 | bytes 6356992 | tf_op jit(solution)/shard_map/dot_general | solution.py:188
  161.4 3.4 %psum.21 = f32[64,128]{1,0:T(8,128)S(1)} all-reduce(f32[64,128]{1,0:T(8,128)S(1)} %fusion.50), channel_id=1, replica_groups=mesh['dp'=2,'context_0'=4,'context_1'=8,'tensor'=4] {'dp'}, use_global_device_ids=true, to_apply=%region_6.7 | all-reduce | flops 8192 | bytes 65536 | tf_op jit(solution)/shard_map/psum | solution.py:54
  164.8 17.3 %psum.22 = f32[64,128]{1,0:T(8,128)S(1)} all-reduce(f32[64,128]{1,0:T(8,128)S(1)} %psum.21), channel_id=1, replica_groups=mesh['dp'=2,'context_0'=4,'context_1'=8,'tensor'=4] {'context_0'}, use_global_device_ids=true, to_apply=%region_7.8 | all-reduce | flops 8192 | bytes 65536 | tf_op jit(solution)/shard_map/psum | solution.py:54
  182.1 30.2 %psum.23 = f32[64,128]{1,0:T(8,128)} all-reduce(f32[64,128]{1,0:T(8,128)S(1)} %psum.22), channel_id=1, replica_groups=mesh['dp'=2,'context_0'=4,'context_1'=8,'tensor'=4] {'context_1'}, use_global_device_ids=true, to_apply=%region_8.9 | all-reduce | flops 8192 | bytes 65536 | tf_op jit(solution)/shard_map/psum | solution.py:54
  (123 shorter events, 55.4 us)
Async XLA Ops:
  0.6 19.3 %copy-start = (bf16[64,128]{1,0:T(8,128)(2,1)S(1)}, bf16[64,128]{1,0:T(8,128)(2,1)}, u32[]{:S(2)}) copy-start(bf16[64,128]{1,0:T(8,128)(2,1)} %param.11) | copy-start | bytes 49156
  0.6 4.2 %copy-start.11 = (bf16[1,256,1024]{2,1,0:T(8,128)(2,1)S(1)}, bf16[1,256,1024]{2,1,0:T(8,128)(2,1)}, u32[]{:S(2)}) copy-start(bf16[1,256,1024]{2,1,0:T(8,128)(2,1)} %param.8) | copy-start | bytes 1572868
  2.6 4.2 %copy-start.13 = (s32[32,32]{1,0:T(8,128)}, s32[32,32]{1,0:T(8,128)S(1)}, u32[]{:S(2)}) copy-start(s32[32,32]{1,0:T(8,128)S(1)} %reshape_squeeze.6) | copy-start | bytes 12292
  4.6 14.2 %copy-start.21 = (s32[1,32]{1,0:T(1,128)S(1)}, s32[1,32]{1,0:T(1,128)}, u32[]{:S(2)}) copy-start(s32[1,32]{1,0:T(1,128)} %param.13) | copy-start | bytes 388
  6.8 44.5 %all-to-all-start = ((bf16[32,8,2048]{2,1,0:T(8,128)(2,1)}), bf16[32,8,2048]{2,1,0:T(8,128)(2,1)}, u32[]{:S(2)}, u32[]{:S(2)}) async-start(bf16[32,8,2048]{2,1,0:T(8,128)(2,1)} %pad_maximum_fusion), calls=%async_computation | async-start | bytes 2097152 | tf_op jit(solution)/shard_map/all_to_all | solution.py:15
  35.0 5.5 %copy-start.14 = (s32[32,32]{1,0:T(8,128)S(1)}, s32[32,32]{1,0:T(8,128)}, u32[]{:S(2)}) copy-start(s32[32,32]{1,0:T(8,128)} %copy-done.13) | copy-start | bytes 12292
  35.0 5.6 %copy-start.2 = (bf16[8,8,256,128]{3,2,1,0:T(8,128)(2,1)S(1)}, bf16[8,8,256,128]{3,2,1,0:T(8,128)(2,1)}, u32[]{:S(2)}) copy-start(bf16[8,8,256,128]{3,2,1,0:T(8,128)(2,1)} %copy.95) | copy-start | bytes 12582916
  40.6 18.6 %copy-start.15 = (s32[32]{0:T(128)}, s32[32]{0:T(128)S(1)}, u32[]{:S(2)}) copy-start(s32[32]{0:T(128)S(1)} %fusion.81) | copy-start | bytes 388
  52.8 29.9 %all-to-all-start.2 = ((bf16[4,256,1024]{1,2,0:T(8,128)(2,1)}), bf16[4,256,1024]{1,2,0:T(8,128)(2,1)}, u32[]{:S(2)}, u32[]{:S(2)}) async-start(bf16[4,256,1024]{1,2,0:T(8,128)(2,1)} %broadcast_in_dim.14), calls=%async_computation.2 | async-start | bytes 4194304 | tf_op jit(solution)/shard_map/all_to_all | solution.py:38
  59.3 9.4 %copy-start.20 = (bf16[384]{0:T(512)(128)(2,1)S(1)}, bf16[384]{0:T(512)(128)(2,1)}, u32[]{:S(2)}) copy-start(bf16[384]{0:T(512)(128)(2,1)} %pad.7.clone) | copy-start | bytes 2308
  60.2 8.5 %collective-permute-start = (bf16[127,1024]{0,1:T(8,128)(2,1)S(1)}, bf16[127,1024]{0,1:T(8,128)(2,1)S(1)}, u32[]{:S(2)}, u32[]{:S(2)}) collective-permute-start(bf16[127,1024]{0,1:T(8,128)(2,1)S(1)} %slice.71), channel_id=1, source_target_pairs={{0,4},{4,8},{8,12},{12,16},{16,20},{20,24},{24,28},{28,32},{32,36}... | collective-permute-start | bytes 780296 | tf_op jit(solution)/shard_map/ppermute | solution.py:22
  65.5 17.2 %copy-start.9 = (f32[256,1024]{1,0:T(8,128)}, f32[256,1024]{1,0:T(8,128)S(1)}, u32[]{:S(2)}) copy-start(f32[256,1024]{1,0:T(8,128)S(1)} %reshape.225) | copy-start | bytes 3145732
  82.7 9.7 %copy-start.10 = (f32[1024,256]{0,1:T(8,128)S(1)}, f32[1024,256]{0,1:T(8,128)}, u32[]{:S(2)}) copy-start(f32[1024,256]{0,1:T(8,128)} %copy.70) | copy-start | bytes 3145732
  90.2 8.3 %copy-start.7 = (bf16[256,1024]{1,0:T(8,128)(2,1)}, bf16[256,1024]{1,0:T(8,128)(2,1)S(1)}, u32[]{:S(2)}) copy-start(bf16[256,1024]{1,0:T(8,128)(2,1)S(1)} %get-tuple-element.10) | copy-start | bytes 1572868
  91.0 8.8 %copy-start.16 = (s32[32]{0:T(128)S(1)}, s32[32]{0:T(128)}, u32[]{:S(2)}) copy-start(s32[32]{0:T(128)} %copy-done.15) | copy-start | bytes 388
  91.0 16.8 %collective-permute-start.1 = (bf16[127,1024]{1,0:T(8,128)(2,1)}, bf16[127,1024]{1,0:T(8,128)(2,1)}, u32[]{:S(2)}, u32[]{:S(2)}) collective-permute-start(bf16[127,1024]{1,0:T(8,128)(2,1)} %slice.76), channel_id=1, source_target_pairs={{4,0},{8,4},{12,8},{16,12},{20,16},{24,20},{28,24},{32,28},{36,32}... | collective-permute-start | bytes 780296 | tf_op jit(solution)/shard_map/ppermute | solution.py:22
  101.3 6.6 %copy-start.8 = (bf16[256,1024]{1,0:T(8,128)(2,1)S(1)}, bf16[256,1024]{1,0:T(8,128)(2,1)}, u32[]{:S(2)}) copy-start(bf16[256,1024]{1,0:T(8,128)(2,1)} %copy-done.7) | copy-start | bytes 1572868
  101.3 6.6 %copy-start.19 = (bf16[384]{0:T(512)(128)(2,1)S(1)}, bf16[384]{0:T(512)(128)(2,1)}, u32[]{:S(2)}) copy-start(bf16[384]{0:T(512)(128)(2,1)} %pad.6.clone) | copy-start | bytes 2308
  102.9 28.9 %all-to-all-start.1 = ((bf16[4,256,1024]{2,1,0:T(8,128)(2,1)}), bf16[4,256,1024]{2,1,0:T(8,128)(2,1)S(1)}, u32[]{:S(2)}, u32[]{:S(2)}) async-start(bf16[4,256,1024]{2,1,0:T(8,128)(2,1)} %bitcast.134), calls=%async_computation.1 | async-start | bytes 4194304 | tf_op jit(solution)/shard_map/all_to_all | solution.py:32
  131.8 81.8 %all-to-all-start.3 = ((bf16[32,8,2048]{2,1,0:T(8,128)(2,1)}), bf16[32,8,2048]{2,1,0:T(8,128)(2,1)}, u32[]{:S(2)}, u32[]{:S(2)}) async-start(bf16[32,8,2048]{2,1,0:T(8,128)(2,1)} %pad_maximum_fusion.1), calls=%async_computation.3 | async-start | bytes 2097152 | tf_op jit(solution)/shard_map/all_to_all | solution.py:15
  161.4 54.6 %copy-start.18 = (s32[32]{0:T(128)S(1)}, s32[32]{0:T(128)}, u32[]{:S(2)}) copy-start(s32[32]{0:T(128)} %copy-done.17) | copy-start | bytes 388
  212.3 4.2 %copy-start.5 = (bf16[1,256,1024]{2,1,0:T(8,128)(2,1)S(1)}, bf16[1,256,1024]{2,1,0:T(8,128)(2,1)}, u32[]{:S(2)}) copy-start(bf16[1,256,1024]{2,1,0:T(8,128)(2,1)} %param.10) | copy-start | bytes 1572868
  212.3 4.2 %copy-start.6 = (bf16[1,256,1024]{2,1,0:T(8,128)(2,1)S(1)}, bf16[1,256,1024]{2,1,0:T(8,128)(2,1)}, u32[]{:S(2)}) copy-start(bf16[1,256,1024]{2,1,0:T(8,128)(2,1)} %param.9) | copy-start | bytes 1572868
  216.0 4.5 %copy-start.1 = (bf16[64,128]{1,0:T(8,128)(2,1)S(1)}, bf16[64,128]{1,0:T(8,128)(2,1)}, u32[]{:S(2)}) copy-start(bf16[64,128]{1,0:T(8,128)(2,1)} %param.11) | copy-start | bytes 49156
  (4 other events, 9.2 us)
where the time goes:
time: 224 us; the launch traced here: 221 us
  matrix products  57.4 us (26%)
  blocking collectives  50.9 us (23%)
  starting transfers between devices  37.8 us (17%)
  local copies, waits for them, and re-layouts  37.6 us (17%)
  other arithmetic  26.2 us (12%)
  waiting for transfers between devices  9.28 us (4%)
    psum x3, blocking collectives, over_axes(): shard = lax.psum(shard, axis)  50.9 us
    all_to_all x2, starting transfers between devices, sent_together(): lax.all_to_all(both, axis, split_axis=split_dim, concat_axis=concat_dim,...  22.6 us
    unnamed x55, local copies, waits for them, and re-layouts  14.4 us
    dot_general x2, matrix products, band_matrix(): jnp.dot(filters, tap_table.reshape(taps, -1), preferred_element_type=jnp....  9.74 us
    dot_general x1, matrix products, per_device(): lax.dot_general(collect(out_grad[0], 'tensor', 1), out_weight, (((1,), (1...  7.49 us
    dot_general x1, matrix products, per_device(): lax.dot_general(summed_tail, table_tail, dims, precision=lax.Precision.HI...  6.78 us
    dot_general x1, matrix products, per_device(): lax.dot_general(summed_head, table_head, dims, precision=lax.Precision.HI...  6.4 us
    dot_general x1, matrix products, per_device(): jnp.dot(gated, out_weight, preferred_element_type=jnp.float32)  6.09 us
  transfers between devices with their start and end apart: 6, of which 3 were waited for; matrix products, arithmetic and copies ran while one was open for 44% of the time, Pallas kernels for 0%

commit v1 on v0

--- a/solution.py
+++ b/solution.py
@@ -51,7 +51,7 @@
 
 def over_axes(shard, axes):
     for axis in axes:
-        shard = lax.psum(shard, axis)
+        shard = jnp.sum(lax.all_gather(shard, axis), axis=0)
     return shard
 
 

time: 224 us -> 215 us (0.960)
  the two profiles are of different devices: /device:TPU:8 before, /device:TPU:2 now
where the time goes in v1:
time: 215 us; the launch traced here: 211 us
  matrix products  57.4 us (27%)
  blocking collectives  39.7 us (18%)
  local copies, waits for them, and re-layouts  37.6 us (17%)
  starting transfers between devices  36.6 us (17%)
  other arithmetic  26.9 us (13%)
  waiting for transfers between devices  11.7 us (5%)
    all_gather x3, blocking collectives, over_axes(): shard = jnp.sum(lax.all_gather(shard, axis), axis=0)  39.7 us
    all_to_all x2, starting transfers between devices, sent_together(): lax.all_to_all(both, axis, split_axis=split_dim, concat_axis=concat_dim,...  20.3 us
    unnamed x55, local copies, waits for them, and re-layouts  14.4 us
    dot_general x2, matrix products, band_matrix(): jnp.dot(filters, tap_table.reshape(taps, -1), preferred_element_type=jnp....  9.74 us
    ppermute x2, starting transfers between devices, from_behind(): lax.ppermute(value, axis, [(source, source + steps) for source in range(f...  8.25 us
    dot_general x1, matrix products, per_device(): lax.dot_general(collect(out_grad[0], 'tensor', 1), out_weight, (((1,), (1...  7.49 us
    dot_general x1, matrix products, per_device(): lax.dot_general(summed_tail, table_tail, dims, precision=lax.Precision.HI...  6.78 us
    ppermute x2, waiting for transfers between devices, from_behind(): lax.ppermute(value, axis, [(source, source + steps) for source in range(f...  6.54 us
  transfers between devices with their start and end apart: 6, of which 3 were waited for; matrix products, arithmetic and copies ran while one was open for 47% of the time, Pallas kernels for 0%

profile of v1, /device:TPU:2, one launch (start us, length us, event | category | flops | bytes accessed | tf_op | source)
XLA Modules:
  0.0 211.4 jit_solution(12503485461551664927)
XLA Ops:
  6.8 12.4 %all-to-all-start = ((bf16[32,8,2048]{2,1,0:T(8,128)(2,1)}), bf16[32,8,2048]{2,1,0:T(8,128)(2,1)}, u32[]{:S(2)}, u32[]{:S(2)}) async-start(bf16[32,8,2048]{2,1,0:T(8,128)(2,1)} %pad_maximum_fusion), calls=%async_computation | async-start | bytes 2097152 | tf_op jit(solution)/shard_map/all_to_all | solution.py:15
  20.4 3.9 %fusion.18 = bf16[8,8,256,128]{3,1,2,0:T(8,128)(2,1)S(1)} fusion(bf16[64,128]{1,0:T(8,128)(2,1)S(1)} %copy-done, s32[32768]{0:T(1024)S(1)} %get-tuple-element.23), kind=kOutput, calls=%fused_computation.36 | convolution fusion | flops 543162368 | bytes 4341760 | tf_op jit(solution)/shard_map/dot_general | solution.py:73
  25.1 5.9 %fusion.19 = bf16[8,8,256,128]{3,1,2,0:T(8,128)(2,1)} fusion(bf16[64,128]{1,0:T(8,128)(2,1)S(1)} %copy-done, s32[32768]{0:T(1024)S(1)} %fusion.77), kind=kOutput, calls=%fused_computation.37 | convolution fusion | flops 543162368 | bytes 4341760 | tf_op jit(solution)/shard_map/dot_general | solution.py:73
  32.1 3.1 %copy.95 = bf16[8,8,256,128]{3,2,1,0:T(8,128)(2,1)} copy(bf16[8,8,256,128]{3,1,2,0:T(8,128)(2,1)S(1)} %fusion.18) | data formatting | bytes 8388608
  35.5 5.4 %copy.98 = bf16[8,8,256,128]{3,2,1,0:T(8,128)(2,1)} copy(bf16[8,8,256,128]{3,1,2,0:T(8,128)(2,1)} %fusion.19) | data formatting | bytes 8388608
  41.0 4.7 %broadcast_multiply_fusion.1 = bf16[2,64,256,128]{3,2,0,1:T(8,128)(2,1)} fusion(bf16[2,256,128]{2,1,0:T(8,128)(2,1)} %get-tuple-element.20, bf16[64,256,128]{2,1,0:T(8,128)(2,1)S(1)} %bitcast.135), kind=kLoop, calls=%fused_computation.35 | loop fusion | flops 4194304 | bytes 12713984 | tf_op jit(solution)/shard_map/mul | solution.py:130
  45.7 6.0 %broadcast_multiply_fusion = bf16[2,64,256,128]{3,2,0,1:T(8,128)(2,1)} fusion(bf16[2,256,128]{2,1,0:T(8,128)(2,1)} %compare_convert_fusion.2, bf16[64,256,128]{2,1,0:T(8,128)(2,1)} %bitcast.136), kind=kLoop, calls=%fused_computation.34 | loop fusion | flops 4194304 | bytes 12713984 | tf_op jit(solution)/shard_map/mul | solution.py:156
  53.2 4.5 %all-to-all-start.2 = ((bf16[4,256,1024]{1,2,0:T(8,128)(2,1)}), bf16[4,256,1024]{1,2,0:T(8,128)(2,1)}, u32[]{:S(2)}, u32[]{:S(2)}) async-start(bf16[4,256,1024]{1,2,0:T(8,128)(2,1)} %broadcast_in_dim.14), calls=%async_computation.2 | async-start | bytes 4194304 | tf_op jit(solution)/shard_map/all_to_all | solution.py:38
  60.1 3.5 %collective-permute-start = (bf16[127,1024]{0,1:T(8,128)(2,1)S(1)}, bf16[127,1024]{0,1:T(8,128)(2,1)S(1)}, u32[]{:S(2)}, u32[]{:S(2)}) collective-permute-start(bf16[127,1024]{0,1:T(8,128)(2,1)S(1)} %slice.71), channel_id=1, source_target_pairs={{0,4},{4,8},{8,12},{12,16},{16,20},{20,24},{24,28},{28,32},{32,36}... | collective-permute-start | bytes 780296 | tf_op jit(solution)/shard_map/ppermute | solution.py:22
  65.1 6.5 %collective-permute-done = bf16[127,1024]{0,1:T(8,128)(2,1)S(1)} collective-permute-done((bf16[127,1024]{0,1:T(8,128)(2,1)S(1)}, bf16[127,1024]{0,1:T(8,128)(2,1)S(1)}, u32[]{:S(2)}, u32[]{:S(2)}) %collective-permute-start) | collective-permute-done | bytes 260128 | tf_op jit(solution)/shard_map/ppermute | solution.py:22
  72.9 3.4 %fusion.12 = f32[64,2,128,16]{2,3,1,0:T(8,128)S(1)} fusion(bf16[2,64,256,128]{3,2,0,1:T(8,128)(2,1)} %broadcast_multiply_fusion.1, bf16[64,2,2,8,128]{4,3,2,1,0:T(8,128)(2,1)S(1)} %get-tuple-element.16), kind=kOutput, calls=%fused_computation.28 | convolution fusion | flops 67108864 | bytes 5767168 | tf_op jit(solution)/shard_map/gcks,kgst->gckt/dot_general | solution.py:134
  76.3 3.4 %fusion.23 = f32[64,16,2,128]{3,1,2,0:T(8,128)S(1)} fusion(f32[64,2,128,16]{2,3,1,0:T(8,128)S(1)} %fusion.12, bf16[2,64,256,128]{3,2,0,1:T(8,128)(2,1)} %broadcast_multiply_fusion.1, bf16[64,2,2,8,128]{4,3,2,1,0:T(8,128)(2,1)S(1)} %get-tuple-element.15), kind=kOutput, calls=%fused_computation.40 | convolution fusion | flops 67371008 | bytes 6815744 | tf_op jit(solution)/shard_map/gcks,kgst->gckt/dot_general | solution.py:131
  83.8 7.5 %fusion.59 = (bf16[256,1024]{1,0:T(8,128)(2,1)}, bf16[256,1024]{1,0:T(8,128)(2,1)S(1)}) fusion(f32[1024,256]{0,1:T(8,128)} %copy.70, f32[256,1024]{1,0:T(8,128)S(1)} %reshape.225, bf16[256,4096]{0,1:T(8,128)(2,1)} %bitcast.16, bf16[1024,4096]{1,0:T(8,128)(2,1)} %param.12), kind=kOutput, calls=%fused_computation.60 | convolution fusion | flops 2148532224 | bytes 13631488 | tf_op jit(solution)/shard_map/dot_general | solution.py:143
  92.1 4.7 %collective-permute-start.1 = (bf16[127,1024]{1,0:T(8,128)(2,1)}, bf16[127,1024]{1,0:T(8,128)(2,1)}, u32[]{:S(2)}, u32[]{:S(2)}) collective-permute-start(bf16[127,1024]{1,0:T(8,128)(2,1)} %slice.76), channel_id=1, source_target_pairs={{4,0},{8,4},{12,8},{16,12},{20,16},{24,20},{28,24},{32,28},{36,32}... | collective-permute-start | bytes 780296 | tf_op jit(solution)/shard_map/ppermute | solution.py:22
  96.8 6.1 %convolution_convert_fusion.10 = bf16[256,4096]{1,0:T(8,128)(2,1)S(1)} fusion(bf16[1024,4096]{1,0:T(8,128)(2,1)} %param.12, f32[256,1024]{1,0:T(8,128)} %copy-done.9, f32[1024,256]{0,1:T(8,128)S(1)} %copy-done.10), kind=kOutput, calls=%fused_computation.23 | convolution fusion | flops 2149056512 | bytes 12582912 | tf_op jit(solution)/shard_map/dot_general | solution.py:139
  107.3 3.6 %all-to-all-start.1 = ((bf16[4,256,1024]{2,1,0:T(8,128)(2,1)}), bf16[4,256,1024]{2,1,0:T(8,128)(2,1)S(1)}, u32[]{:S(2)}, u32[]{:S(2)}) async-start(bf16[4,256,1024]{2,1,0:T(8,128)(2,1)} %bitcast.137), calls=%async_computation.1 | async-start | bytes 4194304 | tf_op jit(solution)/shard_map/all_to_all | solution.py:32
  116.6 3.4 %fusion.8 = f32[64,2,128,16]{2,3,1,0:T(8,128)S(1)} fusion(bf16[2,64,256,128]{3,2,0,1:T(8,128)(2,1)} %broadcast_multiply_fusion, bf16[64,2,2,8,128]{4,3,2,1,0:T(8,128)(2,1)S(1)} %get-tuple-element.14), kind=kOutput, calls=%fused_computation.24 | convolution fusion | flops 67108864 | bytes 5767168 | tf_op jit(solution)/shard_map/gckt,kgts->gcks/dot_general | solution.py:160
  120.0 3.4 %fusion.32 = bf16[64,16,2,128]{3,1,2,0:T(8,128)(2,1)S(1)} fusion(f32[64,2,128,16]{2,3,1,0:T(8,128)S(1)} %fusion.8, bf16[2,64,256,128]{3,2,0,1:T(8,128)(2,1)} %broadcast_multiply_fusion, bf16[64,2,2,8,128]{4,3,2,1,0:T(8,128)(2,1)S(1)} %get-tuple-element.13), kind=kOutput, calls=%fused_computation.46 | convolution fusion | flops 67633152 | bytes 6291456 | tf_op jit(solution)/shard_map/gckt,kgts->gcks/dot_general | solution.py:157
  132.6 3.1 %all-to-all-done.1 = bf16[4,256,1024]{2,1,0:T(8,128)(2,1)S(1)} async-done(((bf16[4,256,1024]{2,1,0:T(8,128)(2,1)}), bf16[4,256,1024]{2,1,0:T(8,128)(2,1)S(1)}, u32[]{:S(2)}, u32[]{:S(2)}) %all-to-all-start.1) | async-done | bytes 2097184 | tf_op jit(solution)/shard_map/all_to_all | solution.py:32
  135.7 7.9 %all-to-all-start.3 = ((bf16[32,8,2048]{2,1,0:T(8,128)(2,1)}), bf16[32,8,2048]{2,1,0:T(8,128)(2,1)}, u32[]{:S(2)}, u32[]{:S(2)}) async-start(bf16[32,8,2048]{2,1,0:T(8,128)(2,1)} %pad_maximum_fusion.1), calls=%async_computation.3 | async-start | bytes 2097152 | tf_op jit(solution)/shard_map/all_to_all | solution.py:15
  149.5 6.4 %fusion.35 = f32[64,128]{1,0:T(8,128)S(1)} fusion(pred[128,256,128]{2,0,1:T(32,128)(4,1)S(1)} %iota_compare_fusion, f32[64,128,128]{2,1,0:T(8,128)S(1)} %multiply_reduce_fusion.1), kind=kOutput, calls=%fused_computation.47 | convolution fusion | flops 1610612736 | bytes 6324224 | tf_op jit(solution)/shard_map/dot_general | solution.py:181
  155.9 6.8 %fusion.50 = f32[64,128]{1,0:T(8,128)S(1)} fusion(f32[64,128]{1,0:T(8,128)S(1)} %fusion.35, pred[128,256,128]{2,0,1:T(32,128)(4,1)S(1)} %iota_compare_fusion, f32[64,128,128]{2,1,0:T(8,128)S(1)} %multiply_reduce_fusion), kind=kOutput, calls=%fused_computation.50 | convolution fusion | flops 1610629120 | bytes 6356992 | tf_op jit(solution)/shard_map/dot_general | solution.py:188
  164.5 12.2 %all-gather.1 = f32[256,128]{1,0:T(8,128)S(1)} all-gather(f32[64,128]{1,0:T(8,128)S(1)} %reduce_sum.70), channel_id=3, replica_groups=mesh['dp'=2,'context_0'=4,'context_1'=8,'tensor'=4] {'context_0'}, dimensions={0}, use_global_device_ids=true | all-gather | bytes 163840 | tf_op jit(solution)/shard_map/all_gather | solution.py:54
  176.7 25.7 %all-gather.2 = f32[512,128]{1,0:T(8,128)S(1)} all-gather(f32[64,128]{1,0:T(8,128)S(1)} %reduce_sum.71), channel_id=4, replica_groups=mesh['dp'=2,'context_0'=4,'context_1'=8,'tensor'=4] {'context_1'}, dimensions={0}, use_global_device_ids=true | all-gather | bytes 294912 | tf_op jit(solution)/shard_map/all_gather | solution.py:54
  (126 shorter events, 56.3 us)
Async XLA Ops:
  0.6 19.7 %copy-start = (bf16[64,128]{1,0:T(8,128)(2,1)S(1)}, bf16[64,128]{1,0:T(8,128)(2,1)}, u32[]{:S(2)}) copy-start(bf16[64,128]{1,0:T(8,128)(2,1)} %param.11) | copy-start | bytes 49156
  0.6 4.2 %copy-start.11 = (bf16[1,256,1024]{2,1,0:T(8,128)(2,1)S(1)}, bf16[1,256,1024]{2,1,0:T(8,128)(2,1)}, u32[]{:S(2)}) copy-start(bf16[1,256,1024]{2,1,0:T(8,128)(2,1)} %param.8) | copy-start | bytes 1572868
  2.6 4.2 %copy-start.13 = (s32[32,32]{1,0:T(8,128)}, s32[32,32]{1,0:T(8,128)S(1)}, u32[]{:S(2)}) copy-start(s32[32,32]{1,0:T(8,128)S(1)} %reshape_squeeze.6) | copy-start | bytes 12292
  4.6 14.7 %copy-start.21 = (s32[1,32]{1,0:T(1,128)S(1)}, s32[1,32]{1,0:T(1,128)}, u32[]{:S(2)}) copy-start(s32[1,32]{1,0:T(1,128)} %param.13) | copy-start | bytes 388
  6.8 44.9 %all-to-all-start = ((bf16[32,8,2048]{2,1,0:T(8,128)(2,1)}), bf16[32,8,2048]{2,1,0:T(8,128)(2,1)}, u32[]{:S(2)}, u32[]{:S(2)}) async-start(bf16[32,8,2048]{2,1,0:T(8,128)(2,1)} %pad_maximum_fusion), calls=%async_computation | async-start | bytes 2097152 | tf_op jit(solution)/shard_map/all_to_all | solution.py:15
  35.4 5.5 %copy-start.14 = (s32[32,32]{1,0:T(8,128)S(1)}, s32[32,32]{1,0:T(8,128)}, u32[]{:S(2)}) copy-start(s32[32,32]{1,0:T(8,128)} %copy-done.13) | copy-start | bytes 12292
  35.5 5.6 %copy-start.2 = (bf16[8,8,256,128]{3,2,1,0:T(8,128)(2,1)S(1)}, bf16[8,8,256,128]{3,2,1,0:T(8,128)(2,1)}, u32[]{:S(2)}) copy-start(bf16[8,8,256,128]{3,2,1,0:T(8,128)(2,1)} %copy.95) | copy-start | bytes 12582916
  41.0 18.2 %copy-start.15 = (s32[32]{0:T(128)}, s32[32]{0:T(128)S(1)}, u32[]{:S(2)}) copy-start(s32[32]{0:T(128)S(1)} %fusion.81) | copy-start | bytes 388
  53.2 30.6 %all-to-all-start.2 = ((bf16[4,256,1024]{1,2,0:T(8,128)(2,1)}), bf16[4,256,1024]{1,2,0:T(8,128)(2,1)}, u32[]{:S(2)}, u32[]{:S(2)}) async-start(bf16[4,256,1024]{1,2,0:T(8,128)(2,1)} %broadcast_in_dim.14), calls=%async_computation.2 | async-start | bytes 4194304 | tf_op jit(solution)/shard_map/all_to_all | solution.py:38
  59.2 12.4 %copy-start.20 = (bf16[384]{0:T(512)(128)(2,1)S(1)}, bf16[384]{0:T(512)(128)(2,1)}, u32[]{:S(2)}) copy-start(bf16[384]{0:T(512)(128)(2,1)} %pad.7.clone) | copy-start | bytes 2308
  60.1 11.5 %collective-permute-start = (bf16[127,1024]{0,1:T(8,128)(2,1)S(1)}, bf16[127,1024]{0,1:T(8,128)(2,1)S(1)}, u32[]{:S(2)}, u32[]{:S(2)}) collective-permute-start(bf16[127,1024]{0,1:T(8,128)(2,1)S(1)} %slice.71), channel_id=1, source_target_pairs={{0,4},{4,8},{8,12},{12,16},{16,20},{20,24},{24,28},{28,32},{32,36}... | collective-permute-start | bytes 780296 | tf_op jit(solution)/shard_map/ppermute | solution.py:22
  65.1 18.7 %copy-start.9 = (f32[256,1024]{1,0:T(8,128)}, f32[256,1024]{1,0:T(8,128)S(1)}, u32[]{:S(2)}) copy-start(f32[256,1024]{1,0:T(8,128)S(1)} %reshape.225) | copy-start | bytes 3145732
  83.8 13.0 %copy-start.10 = (f32[1024,256]{0,1:T(8,128)S(1)}, f32[1024,256]{0,1:T(8,128)}, u32[]{:S(2)}) copy-start(f32[1024,256]{0,1:T(8,128)} %copy.70) | copy-start | bytes 3145732
  91.3 11.6 %copy-start.7 = (bf16[256,1024]{1,0:T(8,128)(2,1)}, bf16[256,1024]{1,0:T(8,128)(2,1)S(1)}, u32[]{:S(2)}) copy-start(bf16[256,1024]{1,0:T(8,128)(2,1)S(1)} %get-tuple-element.10) | copy-start | bytes 1572868
  92.1 12.1 %copy-start.16 = (s32[32]{0:T(128)S(1)}, s32[32]{0:T(128)}, u32[]{:S(2)}) copy-start(s32[32]{0:T(128)} %copy-done.15) | copy-start | bytes 388
  92.1 18.8 %collective-permute-start.1 = (bf16[127,1024]{1,0:T(8,128)(2,1)}, bf16[127,1024]{1,0:T(8,128)(2,1)}, u32[]{:S(2)}, u32[]{:S(2)}) collective-permute-start(bf16[127,1024]{1,0:T(8,128)(2,1)} %slice.76), channel_id=1, source_target_pairs={{4,0},{8,4},{12,8},{16,12},{20,16},{24,20},{28,24},{32,28},{36,32}... | collective-permute-start | bytes 780296 | tf_op jit(solution)/shard_map/ppermute | solution.py:22
  105.7 5.2 %copy-start.8 = (bf16[256,1024]{1,0:T(8,128)(2,1)S(1)}, bf16[256,1024]{1,0:T(8,128)(2,1)}, u32[]{:S(2)}) copy-start(bf16[256,1024]{1,0:T(8,128)(2,1)} %copy-done.7) | copy-start | bytes 1572868
  105.7 5.2 %copy-start.19 = (bf16[384]{0:T(512)(128)(2,1)S(1)}, bf16[384]{0:T(512)(128)(2,1)}, u32[]{:S(2)}) copy-start(bf16[384]{0:T(512)(128)(2,1)} %pad.6.clone) | copy-start | bytes 2308
  107.3 28.4 %all-to-all-start.1 = ((bf16[4,256,1024]{2,1,0:T(8,128)(2,1)}), bf16[4,256,1024]{2,1,0:T(8,128)(2,1)S(1)}, u32[]{:S(2)}, u32[]{:S(2)}) async-start(bf16[4,256,1024]{2,1,0:T(8,128)(2,1)} %bitcast.137), calls=%async_computation.1 | async-start | bytes 4194304 | tf_op jit(solution)/shard_map/all_to_all | solution.py:32
  135.7 68.6 %all-to-all-start.3 = ((bf16[32,8,2048]{2,1,0:T(8,128)(2,1)}), bf16[32,8,2048]{2,1,0:T(8,128)(2,1)}, u32[]{:S(2)}, u32[]{:S(2)}) async-start(bf16[32,8,2048]{2,1,0:T(8,128)(2,1)} %pad_maximum_fusion.1), calls=%async_computation.3 | async-start | bytes 2097152 | tf_op jit(solution)/shard_map/all_to_all | solution.py:15
  162.6 44.0 %copy-start.18 = (s32[32]{0:T(128)S(1)}, s32[32]{0:T(128)}, u32[]{:S(2)}) copy-start(s32[32]{0:T(128)} %copy-done.17) | copy-start | bytes 388
  203.0 4.2 %copy-start.5 = (bf16[1,256,1024]{2,1,0:T(8,128)(2,1)S(1)}, bf16[1,256,1024]{2,1,0:T(8,128)(2,1)}, u32[]{:S(2)}) copy-start(bf16[1,256,1024]{2,1,0:T(8,128)(2,1)} %param.10) | copy-start | bytes 1572868
  203.0 4.2 %copy-start.6 = (bf16[1,256,1024]{2,1,0:T(8,128)(2,1)S(1)}, bf16[1,256,1024]{2,1,0:T(8,128)(2,1)}, u32[]{:S(2)}) copy-start(bf16[1,256,1024]{2,1,0:T(8,128)(2,1)} %param.9) | copy-start | bytes 1572868
  206.6 4.5 %copy-start.1 = (bf16[64,128]{1,0:T(8,128)(2,1)S(1)}, bf16[64,128]{1,0:T(8,128)(2,1)}, u32[]{:S(2)}) copy-start(bf16[64,128]{1,0:T(8,128)(2,1)} %param.11) | copy-start | bytes 49156
  (4 other events, 9.2 us)
